TPU v7x, 256 devices: a whole 4x4x8 slice. The times are simulated.
256 devices in a mesh: dp: 8 (over x, y_lo), seq: 32 (over z, y_hi, core).
Axes of the slice: x: 4, y: 4 (y_hi: 2, y_lo: 2; y = y_hi * 2 + y_lo), z: 8, core: 2. Of those that a mesh axis runs over, the one named last changes fastest.
Arguments:
- video: bfloat16 [8, 32, 16, 160, 256], P('dp', 'seq'), may hold values from -6 to 6
- cotangent: bfloat16 [8, 32, 16, 160, 256], P('dp', 'seq'), may hold values from -6 to 6
- spatial_weight: bfloat16 [3, 3, 256, 256], replicated, may hold values from -0.125 to 0.125
- temporal_weight: bfloat16 [3, 256, 256], replicated, may hold values from -0.21875 to 0.21875
Outputs:
- video_grad: bfloat16 [8, 32, 16, 160, 256], P('dp', 'seq')
- spatial_grad: float32 [2304, 256], P('seq')
- temporal_grad: float32 [768, 256], P('seq')
All inputs are finite; a program needn't handle non-finite values.
Results may differ from a plain program's by a relative error of at most 0.0054.
Values may be sent and summed in bfloat16 or wider, within the bound.
A program may use at most 128 MiB of HBM per device.

v0:
```python
import jax
import jax.numpy as jnp
from jax import lax
from jax.sharding import PartitionSpec as P


def reduce_grads(partial_sum):
    whole = lax.psum(partial_sum, "dp")
    return lax.psum_scatter(whole, "seq", scatter_dimension=0, tiled=True)


def shards(video, cotangent, spatial_weight, temporal_weight):
    height, width, chans = (video.shape[2], video.shape[3], video.shape[4])
    positions = height * width
    frame = video[0, 0]
    padded = jnp.pad(frame, ((1, 1), (1, 1), (0, 0)))
    hidden = jnp.zeros((height, width, chans), jnp.float32)
    for a in range(3):
        for b in range(3):
            hidden = hidden + jnp.einsum(
                "hwc,cd->hwd",
                padded[a : a + height, b : b + width],
                spatial_weight[a, b],
                preferred_element_type=jnp.float32,
            )
    hidden_low = hidden.astype(jnp.bfloat16)
    grad_flat = cotangent[0, 0].reshape(1, positions, chans)
    hidden_flat = hidden_low.reshape(1, positions, chans)
    total_count = lax.axis_size("dp") * video.shape[0] * lax.axis_size("seq") * positions
    scale = 1.0 / jnp.sqrt(jnp.float32(total_count))
    grad_rows, hidden_rows = (
        lax.all_to_all(grad_flat, "seq", split_axis=1, concat_axis=0, tiled=True),
        lax.all_to_all(hidden_flat, "seq", split_axis=1, concat_axis=0, tiled=True),
    )
    frames = grad_rows.shape[0]
    hid32 = hidden_rows.astype(jnp.float32)
    sig = jax.nn.sigmoid(hid32)
    act = (hid32 * sig).astype(jnp.bfloat16)
    grad_pad = jnp.pad(grad_rows, ((0, 2), (0, 0), (0, 0)))
    act_grad = jnp.zeros(hid32.shape, jnp.float32)
    taps = []
    for k in range(3):
        act_grad = act_grad + jnp.einsum(
            "tqd,cd->tqc",
            grad_pad[k : k + frames],
            temporal_weight[k],
            preferred_element_type=jnp.float32,
        )
        taps.append(
            jnp.einsum(
                "tqc,tqd->cd", act[: frames - k], grad_rows[k:], preferred_element_type=jnp.float32
            )
        )
    temporal_part = jnp.concatenate(taps, axis=0)
    grad_rows_h = (act_grad * sig * (1.0 + hid32 * (1.0 - sig))).astype(jnp.bfloat16)
    back_flat = lax.all_to_all(grad_rows_h, "seq", split_axis=0, concat_axis=1, tiled=True)
    hidden_grad = back_flat.reshape(height, width, chans)
    temporal_grad = reduce_grads(temporal_part) * scale
    grad_pad2 = jnp.pad(hidden_grad, ((1, 1), (1, 1), (0, 0)))
    back = jnp.zeros((height, width, chans), jnp.float32)
    parts = []
    for a in range(3):
        for b in range(3):
            back = back + jnp.einsum(
                "hwd,cd->hwc",
                grad_pad2[2 - a : 2 - a + height, 2 - b : 2 - b + width],
                spatial_weight[a, b],
                preferred_element_type=jnp.float32,
            )
            parts.append(
                jnp.einsum(
                    "hwc,hwd->cd",
                    padded[a : a + height, b : b + width],
                    hidden_grad,
                    preferred_element_type=jnp.float32,
                )
            )
    spatial_grad = reduce_grads(jnp.concatenate(parts, axis=0)) * scale
    video_grad = back.astype(jnp.bfloat16).reshape(video.shape)
    return (video_grad, spatial_grad, temporal_grad)


def solution(mesh):
    placed = (P("dp", "seq", None, None, None), P("dp", "seq", None, None, None), P(), P())
    return jax.shard_map(
        shards,
        mesh=mesh,
        in_specs=placed,
        out_specs=(P("dp", "seq", None, None, None), P("seq", None), P("seq", None)),
        check_vma=False,
    )
```

profile of v0, /device:TPU:2, one launch (start us, length us, event | category | flops | bytes accessed | tf_op | source)
XLA Modules:
  0.0 478.6 jit_solution(2925747647652449)
XLA Ops:
  7.2 4.1 copy.19
  11.8 14.1 %reduce.1 = bf16[2560,256]{1,0:T(8,128)(2,1)} reduce(bf16[2560,1,256]{2,1,0:T(2,128)(2,1)S(1)} %bitcast.204, bf16[]{:T(256)} %broadcast.12), dimensions={1}, to_apply=%bitcast.159.reduce_sub_computation | reduce | bytes 2621442
  25.9 4.1 reshape.59
  30.0 11.9 %all-to-all-start = ((bf16[32,2,10240]{2,1,0:T(2,128)(2,1)}), bf16[32,2,10240]{2,1,0:T(2,128)(2,1)}, u32[]{:S(2)}, u32[]{:S(2)}) async-start(bf16[32,2,10240]{2,1,0:T(2,128)(2,1)} %reshape.59), calls=%async_computation | async-start | bytes 2621440 | tf_op jit(solution)/shard_map/all_to_all | solution.py:32
  46.0 2.2 add_convert_fusion.1
  48.2 16.0 %copy.18 = bf16[1,2560,256]{2,0,1:T(2,128)(2,1)} copy(bf16[1,2560,256]{2,1,0:T(8,128)(2,1)S(1)} %bitcast.206) | data formatting | bytes 2621440 | tf_op jit(solution)/shard_map/reshape | solution.py:28
  64.2 14.1 %reduce = bf16[2560,256]{1,0:T(8,128)(2,1)S(1)} reduce(bf16[2560,1,256]{2,1,0:T(2,128)(2,1)} %bitcast.205, bf16[]{:T(256)} %broadcast.12), dimensions={1}, to_apply=%bitcast.158.reduce_sub_computation | reduce | bytes 2621442
  78.3 1.2 reshape.57
  79.6 9.9 %all-to-all-start.1 = ((bf16[32,2,10240]{2,1,0:T(2,128)(2,1)}), bf16[32,2,10240]{2,1,0:T(2,128)(2,1)}, u32[]{:S(2)}, u32[]{:S(2)}) async-start(bf16[32,2,10240]{2,1,0:T(2,128)(2,1)} %reshape.57), calls=%async_computation.1 | async-start | bytes 2621440 | tf_op jit(solution)/shard_map/all_to_all | solution.py:33
  89.5 8.9 %reshape.60 = bf16[2560,1,256]{2,1,0:T(2,128)(2,1)} reshape(bf16[32,2,10240]{2,1,0:T(2,128)(2,1)} %all-to-all-done) | data formatting | bytes 2621440
  98.3 2.0 copy.12
  100.4 2.0 fusion.93
  102.4 2.0 fusion.95
  104.4 18.8 %all-to-all-done.1 = bf16[32,2,10240]{2,1,0:T(2,128)(2,1)} async-done(((bf16[32,2,10240]{2,1,0:T(2,128)(2,1)}), bf16[32,2,10240]{2,1,0:T(2,128)(2,1)}, u32[]{:S(2)}, u32[]{:S(2)}) %all-to-all-start.1) | async-done | bytes 1310752 | tf_op jit(solution)/shard_map/all_to_all | solution.py:33
  123.2 8.9 %reshape.58 = bf16[2560,1,256]{2,1,0:T(2,128)(2,1)} reshape(bf16[32,2,10240]{2,1,0:T(2,128)(2,1)} %all-to-all-done.1) | data formatting | bytes 2621440
  132.1 2.1 copy.13
  134.2 1.5 copy-done.4
  136.1 2.4 multiply_convert_fusion.1
  138.4 5.6 %all-to-all-start.2 = ((bf16[32,80,256]{2,1,0:T(8,128)(2,1)}), bf16[32,80,256]{2,1,0:T(8,128)(2,1)S(1)}, u32[]{:S(2)}, u32[]{:S(2)}) async-start(bf16[32,80,256]{2,1,0:T(8,128)(2,1)} %multiply_convert_fusion.1), calls=%async_computation.2 | async-start | bytes 2621440 | tf_op jit(solution)/shard_map/all_to_all | solution.py:56
  144.1 4.9 %slice.165 = bf16[1,2480,256]{2,0,1:T(2,128)(2,1)S(1)} slice(bf16[1,2560,256]{2,0,1:T(2,128)(2,1)} %bitcast.195), slice={[0:1], [80:2560], [0:256]} | slice | bytes 2539520 | tf_op jit(solution)/shard_map/slice | solution.py:51
  149.0 2.6 slice.166
  152.1 1.5 copy-done.5
  155.4 0.8 copy-done.3
  156.7 0.9 pad_maximum_fusion
  158.0 20.1 %all-to-all-done.2 = bf16[32,80,256]{2,1,0:T(8,128)(2,1)S(1)} async-done(((bf16[32,80,256]{2,1,0:T(8,128)(2,1)}), bf16[32,80,256]{2,1,0:T(8,128)(2,1)S(1)}, u32[]{:S(2)}, u32[]{:S(2)}) %all-to-all-start.2) | async-done | bytes 1310752 | tf_op jit(solution)/shard_map/all_to_all | solution.py:56
  178.1 1.2 fusion.24
  179.3 1.3 fusion.23
  180.6 1.3 fusion.22
  181.8 1.2 fusion.21
  183.1 1.4 fusion.20
  184.4 1.3 fusion.19
  185.7 1.2 fusion.18
  186.9 1.2 fusion.17
  188.2 1.3 fusion.16
  189.5 84.1 %reduce-scatter.5.cloned.1.call-done = f32[24,256]{1,0:T(8,128)} async-done(((f32[768,256]{1,0:T(8,128)}), f32[24,256]{1,0:T(8,128)}) %reduce-scatter.5.cloned.1.call-update) | async-done | bytes 24592 | tf_op jit(solution)/shard_map/reduce_scatter | solution.py:9
  273.6 31.7 %psum.17 = f32[24,256]{1,0:T(8,128)S(1)} all-reduce(f32[24,256]{1,0:T(8,128)} %reduce-scatter.5.cloned.1.call-done), channel_id=1, replica_groups=mesh['dp'=8,'seq'=32] {'dp'}, use_global_device_ids=true, to_apply=%region_2.3 | all-reduce | flops 6144 | bytes 49152 | tf_op jit(solution)/shard_map/psum | solution.py:8
  305.9 2.0 fusion.10
  307.9 2.0 fusion.12
  309.9 2.0 fusion.14
  311.9 2.0 fusion.2
  314.0 2.0 fusion.4
  316.0 2.0 fusion.6
  318.1 2.1 fusion.8
  320.1 2.1 fusion.82
  322.2 74.5 %reduce-scatter.3.cloned.1.call-done = f32[72,256]{1,0:T(8,128)} async-done(((f32[2304,256]{1,0:T(8,128)}), f32[72,256]{1,0:T(8,128)}) %reduce-scatter.3.cloned.1.call-update) | async-done | bytes 73744 | tf_op jit(solution)/shard_map/reduce_scatter | solution.py:9
  396.7 9.3 %fusion = bf16[1,1,16,160,256]{4,3,2,1,0:T(8,128)(2,1)} fusion(f32[16,160,256]{2,1,0:T(8,128)} %fusion.2, f32[16,160,256]{2,1,0:T(8,128)} %fusion.4, f32[16,160,256]{2,1,0:T(8,128)} %fusion.6, f32[16,160,256]{2,1,0:T(8,128)} %fusion.82, f32[16,160,256]{2,1,0:T(8,128)} %fusion.8, f32[16,160,256]{2,1,0:T(8,128)} %fusion.10, f32[16,160,256]{2,1,0:T(8,128)} %fusion.14, ...), kind=kOutput, calls=%fused_computation.5 | convolution fusion | flops 341442560 | bytes 23724032 | tf_op jit(solution)/shard_map/hwd,cd->hwc/dot_general | solution.py:64
  406.0 64.5 %all-reduce.5.cloned.1.call-done = f32[72,256]{1,0:T(8,128)} async-done(((f32[72,256]{1,0:T(8,128)}), f32[72,256]{1,0:T(8,128)}) %all-reduce.5.cloned.1.call-update) | async-done | bytes 73744 | tf_op jit(solution)/shard_map/psum | solution.py:8
  470.5 1.5 broadcast_multiply_fusion
  (42 shorter events, 8.9 us)
Async XLA Ops:
  30.0 11.9 %copy-start = (bf16[1,1,16,160,256]{4,3,2,1,0:T(8,128)(2,1)S(1)}, bf16[1,1,16,160,256]{4,3,2,1,0:T(8,128)(2,1)}, u32[]{:S(2)}) copy-start(bf16[1,1,16,160,256]{4,3,2,1,0:T(8,128)(2,1)} %param.4) | copy-start | bytes 3932164
  30.0 11.9 %copy-start.6 = (bf16[3,3,256,256]{3,2,1,0:T(8,128)(2,1)S(1)}, bf16[3,3,256,256]{3,2,1,0:T(8,128)(2,1)}, u32[]{:S(2)}) copy-start(bf16[3,3,256,256]{3,2,1,0:T(8,128)(2,1)} %param.6) | copy-start | bytes 3538948
  30.0 49.6 %all-to-all-start = ((bf16[32,2,10240]{2,1,0:T(2,128)(2,1)}), bf16[32,2,10240]{2,1,0:T(2,128)(2,1)}, u32[]{:S(2)}, u32[]{:S(2)}) async-start(bf16[32,2,10240]{2,1,0:T(2,128)(2,1)} %reshape.59), calls=%async_computation | async-start | bytes 2621440 | tf_op jit(solution)/shard_map/all_to_all | solution.py:32
  79.6 43.6 %all-to-all-start.1 = ((bf16[32,2,10240]{2,1,0:T(2,128)(2,1)}), bf16[32,2,10240]{2,1,0:T(2,128)(2,1)}, u32[]{:S(2)}, u32[]{:S(2)}) async-start(bf16[32,2,10240]{2,1,0:T(2,128)(2,1)} %reshape.57), calls=%async_computation.1 | async-start | bytes 2621440 | tf_op jit(solution)/shard_map/all_to_all | solution.py:33
  98.3 2.0 copy-start.10
  100.4 33.8 %copy-start.2 = (bf16[1,2560,256]{2,1,0:T(8,128)(2,1)}, bf16[1,2560,256]{2,1,0:T(8,128)(2,1)S(1)}, u32[]{:S(2)}) copy-start(bf16[1,2560,256]{2,1,0:T(8,128)(2,1)S(1)} %copy.12) | copy-start | bytes 3932164
  132.1 3.6 copy-start.8
  132.1 4.0 copy-start.9
  134.2 1.6 copy-start.4
  138.4 39.6 %all-to-all-start.2 = ((bf16[32,80,256]{2,1,0:T(8,128)(2,1)}), bf16[32,80,256]{2,1,0:T(8,128)(2,1)S(1)}, u32[]{:S(2)}, u32[]{:S(2)}) async-start(bf16[32,80,256]{2,1,0:T(8,128)(2,1)} %multiply_convert_fusion.1), calls=%async_computation.2 | async-start | bytes 2621440 | tf_op jit(solution)/shard_map/all_to_all | solution.py:56
  144.0 129.5 %reduce-scatter.5.cloned.1.call-start = ((), (), s32[]{:S(2)}) async-start(), calls=%async_computation.7 | async-start | bytes 811008 | tf_op jit(solution)/shard_map/reduce_scatter | solution.py:9
  144.1 4.9 %copy-start.1 = (bf16[2560,1,256]{2,1,0:T(2,128)(2,1)S(1)}, bf16[2560,1,256]{2,1,0:T(2,128)(2,1)}, u32[]{:S(2)}) copy-start(bf16[2560,1,256]{2,1,0:T(2,128)(2,1)} %reshape.60) | copy-start | bytes 3932164
  151.8 1.7 copy-start.5
  154.9 1.3 copy-start.3
  157.7 239.0 %reduce-scatter.3.cloned.1.call-start = ((), (), s32[]{:S(2)}) async-start(), calls=%async_computation.5 | async-start | bytes 2433024 | tf_op jit(solution)/shard_map/reduce_scatter | solution.py:9
  189.4 116.5 %copy-start.7 = (bf16[3,3,256,256]{3,2,1,0:T(8,128)(2,1)S(1)}, bf16[3,3,256,256]{3,2,1,0:T(8,128)(2,1)}, u32[]{:S(2)}) copy-start(bf16[3,3,256,256]{3,2,1,0:T(8,128)(2,1)} %param.6) | copy-start | bytes 3538948
  189.4 281.1 %all-reduce.5.cloned.1.call-start = ((), (), s32[]{:S(2)}) async-start(), calls=%async_computation.6 | async-start | bytes 147456 | tf_op jit(solution)/shard_map/psum | solution.py:8
Sparse Core Ops, SparseCore 0:
  157.8 115.7 reduce-scatter.4
  278.3 118.3 reduce-scatter.2
  399.3 71.1 all-reduce.4
where the time goes:
time: 480 us; the launch traced here: 479 us
  waiting for transfers between devices  262 us (55%)
  local copies, waits for them, and re-layouts  59.8 us (12%)
  matrix products  51.3 us (11%)
  other arithmetic  32.1 us (7%)
  blocking collectives  31.7 us (7%)
  starting transfers between devices  27.8 us (6%)
  between operations  14 us (3%)
    reduce_scatter x2, waiting for transfers between devices, reduce_grads(): return lax.psum_scatter(whole, 'seq', scatter_dimension=0, tiled=True)  159 us
    psum x1, waiting for transfers between devices, reduce_grads(): whole = lax.psum(partial_sum, 'dp')  64.5 us
    unnamed x31, local copies, waits for them, and re-layouts  32.3 us
    psum x1, blocking collectives, reduce_grads(): whole = lax.psum(partial_sum, 'dp')  31.7 us
    unnamed x2, other arithmetic  28.3 us
    dot_general x9, matrix products, shards(): jnp.einsum('hwd,cd->hwc', grad_pad2[2 - a:2 - a + height, 2 - b:2 - b + w...  25.6 us
    all_to_all x1, waiting for transfers between devices, shards(): lax.all_to_all(grad_rows_h, 'seq', split_axis=0, concat_axis=1, tiled=True)  20.1 us
    all_to_all x1, waiting for transfers between devices, shards(): lax.all_to_all(hidden_flat, 'seq', split_axis=1, concat_axis=0, tiled=True)  18.8 us
  transfers between devices with their start and end apart: 6, of which 5 were waited for; matrix products, arithmetic and copies ran while one was open for 21% of the time, Pallas kernels for 0%

commit v1 on v0

--- a/solution.py
+++ b/solution.py
@@ -5,7 +5,7 @@
 
 
 def reduce_grads(partial_sum):
-    whole = lax.psum(partial_sum, "dp")
+    whole = jnp.sum(lax.all_gather(partial_sum, "dp"), axis=0)
     return lax.psum_scatter(whole, "seq", scatter_dimension=0, tiled=True)
 
 

time: 480 us -> 904 us (1.88)
  waiting for transfers between devices: 262 us -> 692 us
  matrix products: 51.3 us -> 27.4 us
  other arithmetic: 32.1 us -> 46.2 us
  blocking collectives: 31.7 us -> 41.3 us
    all_gather x0 -> x2, waiting for transfers between devices: none -> 453 us  [reduce_grads(): whole = jnp.sum(lax.all_gather(partial_sum, 'dp'), axis=0)]
    reduce_scatter x2, waiting for transfers between devices: 159 us -> 224 us  [reduce_grads(): return lax.psum_scatter(whole, 'seq', scatter_dimension=0, tiled=True)]
    psum x1 -> x0, waiting for transfers between devices: 64.5 us -> none  [reduce_grads(): whole = lax.psum(partial_sum, 'dp')]
    all_to_all x0 -> x1, blocking collectives: none -> 41.3 us  [shards(): lax.all_to_all(grad_rows_h, 'seq', split_axis=0, concat_axis=1, tiled=True)]
    psum x1 -> x0, blocking collectives: 31.7 us -> none  [reduce_grads(): whole = lax.psum(partial_sum, 'dp')]
    all_to_all x1 -> x0, waiting for transfers between devices: 20.1 us -> none  [shards(): lax.all_to_all(grad_rows_h, 'seq', split_axis=0, concat_axis=1, tiled=True)]
    dot_general x9, matrix products: 25.6 us -> 6.7 us  [shards(): jnp.einsum('hwd,cd->hwc', grad_pad2[2 - a:2 - a + height, 2 - b:2 - b + w...]
    reduce_sum x0 -> x2, other arithmetic: none -> 13.5 us  [reduce_grads(): whole = jnp.sum(lax.all_gather(partial_sum, 'dp'), axis=0)]
  transfers between devices with their start and end apart: 6 -> 6, of which waited for: 5 -> 5; matrix products, arithmetic and copies ran while one was open for 21% -> 10% of each run, Pallas kernels for 0% -> 0%
where the time goes in v1:
time: 904 us; the launch traced here: 903 us
  waiting for transfers between devices  692 us (77%)
  local copies, waits for them, and re-layouts  60.4 us (7%)
  other arithmetic  46.2 us (5%)
  blocking collectives  41.3 us (5%)
  matrix products  27.4 us (3%)
  starting transfers between devices  21.9 us (2%)
  between operations  13.9 us (2%)
    all_gather x2, waiting for transfers between devices, reduce_grads(): whole = jnp.sum(lax.all_gather(partial_sum, 'dp'), axis=0)  453 us
    reduce_scatter x2, waiting for transfers between devices, reduce_grads(): return lax.psum_scatter(whole, 'seq', scatter_dimension=0, tiled=True)  224 us
    all_to_all x1, blocking collectives, shards(): lax.all_to_all(grad_rows_h, 'seq', split_axis=0, concat_axis=1, tiled=True)  41.3 us
    unnamed x27, local copies, waits for them, and re-layouts  29.3 us
    unnamed x2, other arithmetic  28.2 us
  transfers between devices with their start and end apart: 6, of which 5 were waited for; matrix products, arithmetic and copies ran while one was open for 10% of the time, Pallas kernels for 0%

profile of v1, /device:TPU:2, one launch (start us, length us, event | category | flops | bytes accessed | tf_op | source)
XLA Modules:
  0.0 902.8 jit_solution(14301364525738051040)
XLA Ops:
  7.2 5.2 copy.19
  12.9 14.1 %reduce.1 = bf16[2560,256]{1,0:T(8,128)(2,1)S(1)} reduce(bf16[2560,1,256]{2,1,0:T(2,128)(2,1)} %bitcast.207, bf16[]{:T(256)} %broadcast.12), dimensions={1}, to_apply=%bitcast.161.reduce_sub_computation | reduce | bytes 2621442
  27.0 1.2 reshape.61
  28.3 11.9 %all-to-all-start = ((bf16[32,2,10240]{2,1,0:T(2,128)(2,1)}), bf16[32,2,10240]{2,1,0:T(2,128)(2,1)}, u32[]{:S(2)}, u32[]{:S(2)}) async-start(bf16[32,2,10240]{2,1,0:T(2,128)(2,1)} %reshape.61), calls=%async_computation | async-start | bytes 2621440 | tf_op jit(solution)/shard_map/all_to_all | solution.py:32
  44.3 1.3 add_convert_fusion.1
  45.6 16.0 %copy.18 = bf16[1,2560,256]{2,0,1:T(2,128)(2,1)} copy(bf16[1,2560,256]{2,1,0:T(8,128)(2,1)S(1)} %bitcast.210) | data formatting | bytes 2621440 | tf_op jit(solution)/shard_map/reshape | solution.py:28
  61.6 14.1 %reduce = bf16[2560,256]{1,0:T(8,128)(2,1)S(1)} reduce(bf16[2560,1,256]{2,1,0:T(2,128)(2,1)} %bitcast.208, bf16[]{:T(256)} %broadcast.12), dimensions={1}, to_apply=%bitcast.160.reduce_sub_computation | reduce | bytes 2621442
  75.7 1.2 reshape.59
  76.9 9.6 %all-to-all-start.1 = ((bf16[32,2,10240]{2,1,0:T(2,128)(2,1)}), bf16[32,2,10240]{2,1,0:T(2,128)(2,1)}, u32[]{:S(2)}, u32[]{:S(2)}) async-start(bf16[32,2,10240]{2,1,0:T(2,128)(2,1)} %reshape.59), calls=%async_computation.1 | async-start | bytes 2621440 | tf_op jit(solution)/shard_map/all_to_all | solution.py:33
  86.8 8.9 reshape.62
  95.7 6.1 slice.165
  101.8 3.9 slice.166
  105.9 14.7 %all-to-all-done.1 = bf16[32,2,10240]{2,1,0:T(2,128)(2,1)} async-done(((bf16[32,2,10240]{2,1,0:T(2,128)(2,1)}), bf16[32,2,10240]{2,1,0:T(2,128)(2,1)}, u32[]{:S(2)}, u32[]{:S(2)}) %all-to-all-start.1) | async-done | bytes 1310752 | tf_op jit(solution)/shard_map/all_to_all | solution.py:33
  120.6 8.9 reshape.60
  129.5 1.9 copy.13
  131.4 0.7 multiply_convert_fusion
  132.1 0.8 copy-done.2
  132.9 1.2 copy-done.4
  134.3 1.5 copy-done.5
  137.1 0.5 convolution_bitcast_fusion.2
  137.7 0.9 pad_maximum_fusion
  139.8 1.2 copy-done.3
  141.0 1.3 multiply_convert_fusion.1
  142.3 41.3 %all_to_all.30 = bf16[32,80,256]{2,1,0:T(8,128)(2,1)S(1)} all-to-all(bf16[32,80,256]{2,1,0:T(8,128)(2,1)S(1)} %multiply_convert_fusion.1), channel_id=1, replica_groups=mesh['dp'=8,'seq'=32] {'seq'}, dimensions={0} | all-to-all | bytes 2621440 | tf_op jit(solution)/shard_map/all_to_all | solution.py:56
  183.6 1.3 fusion.24
  184.9 1.2 fusion.23
  186.2 1.3 fusion.22
  187.4 1.3 fusion.21
  188.7 1.3 fusion.20
  190.0 1.2 fusion.19
  191.2 1.2 fusion.18
  192.5 1.2 fusion.17
  193.7 1.3 fusion.16
  195.1 86.8 %all-gather.7.cloned.1.call-done = f32[6144,256]{1,0:T(8,128)} async-done(((f32[768,256]{1,0:T(8,128)}), f32[6144,256]{1,0:T(8,128)}) %all-gather.7.cloned.1.call-update) | async-done | bytes 6291472 | tf_op jit(solution)/shard_map/all_gather | solution.py:8
  281.9 4.2 reduce_sum.19
  286.1 366.1 %all-gather.5.cloned.1.call-done = f32[18432,256]{1,0:T(8,128)} async-done(((f32[2304,256]{1,0:T(8,128)}), f32[18432,256]{1,0:T(8,128)}) %all-gather.5.cloned.1.call-update) | async-done | bytes 18874384 | tf_op jit(solution)/shard_map/all_gather | solution.py:8
  652.2 9.3 %reduce_sum.18 = f32[2304,256]{1,0:T(8,128)} reduce(f32[8,2304,256]{2,1,0:T(8,128)} %bitcast.203, f32[]{:T(128)} %constant.2.clone.1), dimensions={0}, to_apply=%region_0.1 | reduce | flops 4128768 | bytes 21233668 | tf_op jit(solution)/shard_map/reduce_sum | solution.py:8
  661.5 1.2 copy-done.7
  662.8 0.5 fusion.10
  663.9 0.6 fusion.14
  664.9 0.5 fusion.4
  665.5 0.6 fusion.6
  666.0 0.6 fusion.8
  667.1 2.4 fusion
  669.5 102.3 %reduce-scatter.5.cloned.1.call-done = f32[24,256]{1,0:T(8,128)} async-done(((f32[768,256]{1,0:T(8,128)}), f32[24,256]{1,0:T(8,128)}) %reduce-scatter.5.cloned.1.call-update) | async-done | bytes 24592 | tf_op jit(solution)/shard_map/reduce_scatter | solution.py:9
  771.8 1.3 broadcast_multiply_fusion.1
  773.1 121.6 %reduce-scatter.3.cloned.1.call-done = f32[72,256]{1,0:T(8,128)} async-done(((f32[2304,256]{1,0:T(8,128)}), f32[72,256]{1,0:T(8,128)}) %reduce-scatter.3.cloned.1.call-update) | async-done | bytes 73744 | tf_op jit(solution)/shard_map/reduce_scatter | solution.py:9
  894.8 1.5 broadcast_multiply_fusion
  (41 shorter events, 9.7 us)
Async XLA Ops:
  28.3 11.9 %copy-start = (bf16[1,1,16,160,256]{4,3,2,1,0:T(8,128)(2,1)S(1)}, bf16[1,1,16,160,256]{4,3,2,1,0:T(8,128)(2,1)}, u32[]{:S(2)}) copy-start(bf16[1,1,16,160,256]{4,3,2,1,0:T(8,128)(2,1)} %param.4) | copy-start | bytes 3932164
  28.3 11.9 %copy-start.6 = (bf16[3,3,256,256]{3,2,1,0:T(8,128)(2,1)S(1)}, bf16[3,3,256,256]{3,2,1,0:T(8,128)(2,1)}, u32[]{:S(2)}) copy-start(bf16[3,3,256,256]{3,2,1,0:T(8,128)(2,1)} %param.6) | copy-start | bytes 3538948
  28.3 48.7 %all-to-all-start = ((bf16[32,2,10240]{2,1,0:T(2,128)(2,1)}), bf16[32,2,10240]{2,1,0:T(2,128)(2,1)}, u32[]{:S(2)}, u32[]{:S(2)}) async-start(bf16[32,2,10240]{2,1,0:T(2,128)(2,1)} %reshape.61), calls=%async_computation | async-start | bytes 2621440 | tf_op jit(solution)/shard_map/all_to_all | solution.py:32
  76.9 43.7 %all-to-all-start.1 = ((bf16[32,2,10240]{2,1,0:T(2,128)(2,1)}), bf16[32,2,10240]{2,1,0:T(2,128)(2,1)}, u32[]{:S(2)}, u32[]{:S(2)}) async-start(bf16[32,2,10240]{2,1,0:T(2,128)(2,1)} %reshape.59), calls=%async_computation.1 | async-start | bytes 2621440 | tf_op jit(solution)/shard_map/all_to_all | solution.py:33
  86.6 195.3 %all-gather.7.cloned.1.call-start = ((), (), s32[]{:S(2)}) async-start(), calls=%async_computation.8 | async-start | bytes 7077888 | tf_op jit(solution)/shard_map/all_gather | solution.py:8
  95.7 6.1 copy-start.1
  131.4 1.5 copy-start.2
  131.4 2.7 copy-start.4
  134.1 1.7 copy-start.5
  137.7 1.1 copy-start.8
  138.6 513.6 %all-gather.5.cloned.1.call-start = ((), (), s32[]{:S(2)}) async-start(), calls=%async_computation.7 | async-start | bytes 21233664 | tf_op jit(solution)/shard_map/all_gather | solution.py:8
  139.3 1.7 copy-start.3
  195.0 576.8 %reduce-scatter.5.cloned.1.call-start = ((), (), s32[]{:S(2)}) async-start(), calls=%async_computation.6 | async-start | bytes 811008 | tf_op jit(solution)/shard_map/reduce_scatter | solution.py:9
  286.1 608.7 %reduce-scatter.3.cloned.1.call-start = ((), (), s32[]{:S(2)}) async-start(), calls=%async_computation.5 | async-start | bytes 2433024 | tf_op jit(solution)/shard_map/reduce_scatter | solution.py:9
  661.5 1.3 copy-start.7
Sparse Core Ops, SparseCore 0:
  138.7 143.0 all-gather.6
  283.7 368.5 all-gather.4
  656.2 115.4 reduce-scatter.4
  776.4 118.3 reduce-scatter.2
